TPU v7x, 32 devices: a whole 2x2x4 slice. The times are simulated.
32 devices in a mesh: groups: 2 (over x), chan: 16 (over z, y, core).
Axes of the slice: x: 2, y: 2, z: 4, core: 2. Of those that a mesh axis runs over, the one named last changes fastest.
Arguments:
- spectra: bfloat16 [2, 8, 512, 512], P(None, 'groups', 'chan'), parts along dimension 1, may hold values from -6 to 6
- filter_bank: float32 [2, 8, 65], replicated, may hold values from -0.5 to 0.5
- band_index: int32 [512], replicated, may hold values from 0 to 7
- window_mask: int32 [8, 512], P('groups', 'chan'), parts along dimension 0, may hold values 0 or 1
- owner_order: int32 [8], P('groups'), parts along dimension 0, may hold values from 0 to 15, as said below
- source_offset: int32 [8, 32], P('groups'), parts along dimension 0, may hold values from 0 to 31, each once within a row
Outputs:
- cross: bfloat16 [2, 256, 512, 512], P(None, 'groups', 'chan'), parts along dimension 1
There are 2 independent parts, one for each index of `groups`. A program takes and returns all parts, laid end to end along the dimension named above; an argument that names none is the same for every part. Nothing has to cross between parts.
Inputs may be any that keep to these rules, and one draw needn't show every extreme that they name: `owner_order`: 4 distinct device indices, below 16.
All inputs are finite; a program needn't handle non-finite values. No bound on the sum of `window_mask` on one device may be relied on, other than what follows from the above.
Results may differ from a plain program's by a relative error of at most 0.0057.
Values may be sent and summed in bfloat16 or wider, within the bound.
A program may use at most 192 MiB of HBM per device.

v0:
```python
import jax
import jax.numpy as jnp
from jax import lax
from jax.sharding import PartitionSpec as P

WIN = 4
TAPS = 65
NBANK = 8
SMOOTH = 17
ROUNDS = 4
water_level = 0.05


def padded_2(cells, sides, width):
    for axis, dim in sides:
        count = lax.axis_size(axis)
        ends = count - 1
        head = lax.slice_in_dim(cells, 0, width, axis=dim)
        tail = lax.slice_in_dim(cells, cells.shape[dim] - width, cells.shape[dim], axis=dim)
        cells = jnp.concatenate(
            [
                lax.ppermute(tail, axis, [(i, (i + 1) % count) for i in range(ends)]),
                cells,
                lax.ppermute(head, axis, [((i + 1) % count, i) for i in range(ends)]),
            ],
            axis=dim,
        )
    return cells


def filter_taps(filter_bank, band_index):
    choose = (band_index[:, None] == jnp.arange(NBANK, dtype=jnp.int32)[None, :]).astype(
        jnp.float32
    )
    return jnp.einsum("fb,pbk->pkf", choose, filter_bank, precision=lax.Precision.HIGHEST)


def velocity_whiten(padded, taps, window_mask):
    count = padded.shape[2] - (TAPS - 1)
    out_pos = jnp.arange(count, dtype=jnp.int32)
    in_pos = jnp.arange(padded.shape[2], dtype=jnp.int32)
    tap_pos = jnp.arange(TAPS, dtype=jnp.int32)
    shifter = (in_pos[None, :, None] - out_pos[:, None, None] == tap_pos[None, None, :]).astype(
        jnp.float32
    )
    banded = jnp.einsum("okt,ptf->pfok", shifter, taps, precision=lax.Precision.HIGHEST)
    products = jnp.einsum("pfok,qwkf->pqwof", banded, padded, precision=lax.Precision.HIGHEST)
    real_sum = products[0, 0] - products[1, 1]
    imag_sum = products[0, 1] + products[1, 0]
    power = real_sum * real_sum + imag_sum * imag_sum
    reach = SMOOTH // 2
    bins = jnp.arange(power.shape[2], dtype=jnp.int32)
    window_band = (jnp.abs(bins[:, None] - bins[None, :]) <= reach).astype(jnp.float32)
    smooth = jnp.einsum("wcg,gf->wcf", power, window_band, precision=lax.Precision.HIGHEST) / SMOOTH
    scale = lax.rsqrt(smooth + water_level) * window_mask.astype(jnp.float32)[:, :, None]
    return jnp.stack([real_sum * scale, imag_sum * scale]).astype(jnp.bfloat16)


def cross_block(source, whitened, swapped):
    real_out = jnp.einsum("pwsf,pwcf->scf", source, whitened, preferred_element_type=jnp.float32)
    imag_out = jnp.einsum("pwsf,pwcf->scf", source, swapped, preferred_element_type=jnp.float32)
    return (jnp.stack([real_out, imag_out]) / WIN).astype(jnp.bfloat16)


def body(spectra, filter_bank, band_index, window_mask, owner_order, source_offset):
    half_width = TAPS // 2
    padded = padded_2(spectra, (("chan", 2),), half_width)
    taps = filter_taps(filter_bank, band_index)
    whitened = velocity_whiten(padded.astype(jnp.float32), taps, window_mask)
    swapped = jnp.stack([whitened[1], -whitened[0]])
    positions = jnp.arange(whitened.shape[2], dtype=jnp.int32)

    def own_sources(round_pos):
        choose = (source_offset[round_pos][:, None] == positions[None, :]).astype(jnp.bfloat16)
        picked = jnp.einsum("sc,pwcf->pwsf", choose, whitened, preferred_element_type=jnp.float32)
        return picked.astype(jnp.bfloat16)

    blocks = []
    device_here = lax.axis_index("chan")
    nothing = jnp.zeros((), jnp.float32)
    stacked = jnp.stack(
        [
            jnp.where(
                device_here == owner_order[round_pos],
                own_sources(round_pos).astype(jnp.float32),
                nothing,
            )
            for round_pos in range(ROUNDS)
        ]
    )
    summed = lax.psum(stacked, "chan").astype(jnp.bfloat16)
    for round_pos in range(ROUNDS):
        blocks.append(cross_block(summed[round_pos], whitened, swapped))
    return jnp.concatenate(blocks, axis=1)


def solution(mesh):
    in_specs = (
        P(None, "groups", "chan", None),
        P(),
        P(),
        P("groups", "chan"),
        P("groups"),
        P("groups", None),
    )
    out_specs = P(None, "groups", "chan", None)
    return jax.shard_map(body, mesh=mesh, in_specs=in_specs, out_specs=out_specs, check_vma=False)
```

profile of v0, /device:TPU:0, one launch (start us, length us, event | category | flops | bytes accessed | tf_op | source)
XLA Modules:
  0.0 280.7 jit_solution(10334228674612800739)
XLA Ops:
  0.0 2.5 collective-permute-start
  2.5 1.3 collective-permute-start.1
  4.9 8.0 %convolution_bitcast_fusion = f32[2,512,32,96,1]{1,3,2,0,4:T(8,128)} fusion(f32[2,65,512,1]{2,1,3,0:T(8,128)S(1)} %convolution_bitcast_fusion.10, s32[32,96]{1,0:T(8,128)S(1)} %iota_subtract_fusion), kind=kOutput, calls=%fused_computation.1 | convolution fusion | flops 2453867520 | bytes 12861440 | tf_op jit(solution)/shard_map/okt,ptf->pfok/dot_general | solution.py:46
  14.3 18.0 %copy.108 = f32[2,512,32,96,1]{3,2,0,4,1:T(8,128)} copy(f32[2,512,32,96,1]{1,3,2,0,4:T(8,128)} %convolution_bitcast_fusion) | data formatting | bytes 25165824 | tf_op jit(solution)/shard_map/okt,ptf->pfok/dot_general | solution.py:46
  36.4 49.4 %convolution_bitcast_fusion.9 = f32[2,2,4,32,512]{3,2,0,1,4:T(4,128)} fusion(f32[2,512,32,96,1]{3,2,0,4,1:T(8,128)} %copy.108, bf16[2,4,32,512]{2,1,0,3:T(4,128)(2,1)S(1)} %copy.72, bf16[2,4,32,512]{2,1,0,3:T(4,128)(2,1)S(1)} %copy.71, bf16[2,4,32,512]{2,1,0,3:T(4,128)(2,1)S(1)} %copy.70), kind=kOutput, calls=%fused_computation.18 | convolution fusion | flops 304349184 | bytes 14417920 | tf_op jit(solution)/shard_map/pfok,qwkf->pqwof/dot_general | solution.py:47
  85.8 2.7 multiply_add_fusion
  89.9 2.1 fusion.32
  92.0 2.4 fusion.50
  94.4 1.8 pad_maximum_fusion.2
  96.3 1.5 copy.78
  98.9 1.5 pad_maximum_fusion.1
  100.5 78.1 %all-reduce.1 = bf16[4,2,4,32,512]{4,3,2,1,0:T(8,128)(2,1)S(1)} all-reduce(f32[4,2,4,32,512]{4,3,2,1,0:T(8,128)} %pad_maximum_fusion.1), channel_id=1, replica_groups=mesh['groups'=2,'chan'=16] {'chan'}, use_global_device_ids=true, to_apply=%region_0.1 | all-reduce | flops 524288 | bytes 3145728 | tf_op jit(solution)/shard_map/psum | solution.py:91
  179.4 1.6 copy.118
  181.0 4.3 %convolution_bitcast_fusion.6 = f32[1,32,32,512]{1,2,3,0:T(8,128)} fusion(bf16[2,4,32,512]{2,1,3,0:T(4,128)(2,1)S(1)} %copy.118, bf16[1,4,32,512]{2,1,3,0:T(4,128)(2,1)S(1)} %fusion.32, bf16[1,4,32,512]{2,1,3,0:T(4,128)(2,1)S(1)} %get-tuple-element.6), kind=kOutput, calls=%fused_computation.15 | convolution fusion | flops 8912896 | bytes 2621440 | tf_op jit(solution)/shard_map/pwsf,pwcf->scf/dot_general | solution.py:60
  185.3 4.3 %convolution_bitcast_fusion.5 = f32[1,32,32,512]{1,2,3,0:T(8,128)} fusion(bf16[2,4,32,512]{2,1,3,0:T(4,128)(2,1)S(1)} %copy.118, bf16[1,4,32,512]{2,1,3,0:T(4,128)(2,1)S(1)} %get-tuple-element.5, bf16[1,4,32,512]{2,1,3,0:T(4,128)(2,1)S(1)} %fusion.32), kind=kOutput, calls=%fused_computation.14 | convolution fusion | flops 8912896 | bytes 2621440 | tf_op jit(solution)/shard_map/pwsf,pwcf->scf/dot_general | solution.py:61
  190.3 4.3 %convolution_bitcast_fusion.8 = f32[1,32,32,512]{1,2,3,0:T(8,128)} fusion(bf16[2,4,32,512]{2,1,3,0:T(4,128)(2,1)S(1)} %copy.114, bf16[1,4,32,512]{2,1,3,0:T(4,128)(2,1)S(1)} %fusion.32, bf16[1,4,32,512]{2,1,3,0:T(4,128)(2,1)S(1)} %get-tuple-element.6), kind=kOutput, calls=%fused_computation.17 | convolution fusion | flops 8912896 | bytes 2621440 | tf_op jit(solution)/shard_map/pwsf,pwcf->scf/dot_general | solution.py:60
  194.6 4.3 %convolution_bitcast_fusion.7 = f32[1,32,32,512]{1,2,3,0:T(8,128)} fusion(bf16[2,4,32,512]{2,1,3,0:T(4,128)(2,1)S(1)} %copy.114, bf16[1,4,32,512]{2,1,3,0:T(4,128)(2,1)S(1)} %get-tuple-element.5, bf16[1,4,32,512]{2,1,3,0:T(4,128)(2,1)S(1)} %fusion.32), kind=kOutput, calls=%fused_computation.16 | convolution fusion | flops 8912896 | bytes 2621440 | tf_op jit(solution)/shard_map/pwsf,pwcf->scf/dot_general | solution.py:61
  199.6 4.3 %convolution_bitcast_fusion.2 = f32[1,32,32,512]{1,2,3,0:T(8,128)} fusion(bf16[2,4,32,512]{2,1,3,0:T(4,128)(2,1)S(1)} %copy.126, bf16[1,4,32,512]{2,1,3,0:T(4,128)(2,1)S(1)} %fusion.32, bf16[1,4,32,512]{2,1,3,0:T(4,128)(2,1)S(1)} %get-tuple-element.6), kind=kOutput, calls=%fused_computation.11 | convolution fusion | flops 8912896 | bytes 2621440 | tf_op jit(solution)/shard_map/pwsf,pwcf->scf/dot_general | solution.py:60
  203.9 4.3 %convolution_bitcast_fusion.1 = f32[1,32,32,512]{1,2,3,0:T(8,128)} fusion(bf16[2,4,32,512]{2,1,3,0:T(4,128)(2,1)S(1)} %copy.126, bf16[1,4,32,512]{2,1,3,0:T(4,128)(2,1)S(1)} %get-tuple-element.5, bf16[1,4,32,512]{2,1,3,0:T(4,128)(2,1)S(1)} %fusion.32), kind=kOutput, calls=%fused_computation.10 | convolution fusion | flops 8912896 | bytes 2621440 | tf_op jit(solution)/shard_map/pwsf,pwcf->scf/dot_general | solution.py:61
  208.9 4.3 %convolution_bitcast_fusion.4 = f32[1,32,32,512]{1,2,3,0:T(8,128)} fusion(bf16[2,4,32,512]{2,1,3,0:T(4,128)(2,1)S(1)} %copy.122, bf16[1,4,32,512]{2,1,3,0:T(4,128)(2,1)S(1)} %fusion.32, bf16[1,4,32,512]{2,1,3,0:T(4,128)(2,1)S(1)} %get-tuple-element.6), kind=kOutput, calls=%fused_computation.13 | convolution fusion | flops 8912896 | bytes 2621440 | tf_op jit(solution)/shard_map/pwsf,pwcf->scf/dot_general | solution.py:60
  213.2 4.5 %convolution_bitcast_fusion.3 = f32[1,32,32,512]{1,2,3,0:T(8,128)} fusion(bf16[2,4,32,512]{2,1,3,0:T(4,128)(2,1)S(1)} %copy.122, bf16[1,4,32,512]{2,1,3,0:T(4,128)(2,1)S(1)} %get-tuple-element.5, bf16[1,4,32,512]{2,1,3,0:T(4,128)(2,1)S(1)} %fusion.32), kind=kOutput, calls=%fused_computation.12 | convolution fusion | flops 8912896 | bytes 2621440 | tf_op jit(solution)/shard_map/pwsf,pwcf->scf/dot_general | solution.py:61
  217.7 5.8 %copy.92 = f32[1,32,32,512]{3,2,1,0:T(8,128)S(1)} copy(f32[1,32,32,512]{1,2,3,0:T(8,128)} %convolution_bitcast_fusion.6) | data formatting | bytes 4194304 | tf_op jit(solution)/shard_map/stack | solution.py:62
  223.5 6.6 %copy.93 = f32[1,32,32,512]{3,2,1,0:T(8,128)} copy(f32[1,32,32,512]{1,2,3,0:T(8,128)} %convolution_bitcast_fusion.5) | data formatting | bytes 4194304 | tf_op jit(solution)/shard_map/stack | solution.py:62
  230.1 6.6 %copy.86 = f32[1,32,32,512]{3,2,1,0:T(8,128)} copy(f32[1,32,32,512]{1,2,3,0:T(8,128)} %convolution_bitcast_fusion.8) | data formatting | bytes 4194304 | tf_op jit(solution)/shard_map/stack | solution.py:62
  236.7 6.6 %copy.87 = f32[1,32,32,512]{3,2,1,0:T(8,128)} copy(f32[1,32,32,512]{1,2,3,0:T(8,128)} %convolution_bitcast_fusion.7) | data formatting | bytes 4194304 | tf_op jit(solution)/shard_map/stack | solution.py:62
  243.4 6.6 %copy.104 = f32[1,32,32,512]{3,2,1,0:T(8,128)} copy(f32[1,32,32,512]{1,2,3,0:T(8,128)} %convolution_bitcast_fusion.2) | data formatting | bytes 4194304 | tf_op jit(solution)/shard_map/stack | solution.py:62
  250.0 6.7 %copy.105 = f32[1,32,32,512]{3,2,1,0:T(8,128)} copy(f32[1,32,32,512]{1,2,3,0:T(8,128)} %convolution_bitcast_fusion.1) | data formatting | bytes 4194304 | tf_op jit(solution)/shard_map/stack | solution.py:62
  256.7 6.6 %copy.98 = f32[1,32,32,512]{3,2,1,0:T(8,128)} copy(f32[1,32,32,512]{1,2,3,0:T(8,128)} %convolution_bitcast_fusion.4) | data formatting | bytes 4194304 | tf_op jit(solution)/shard_map/stack | solution.py:62
  263.3 6.6 %copy.99 = f32[1,32,32,512]{3,2,1,0:T(8,128)} copy(f32[1,32,32,512]{1,2,3,0:T(8,128)} %convolution_bitcast_fusion.3) | data formatting | bytes 4194304 | tf_op jit(solution)/shard_map/stack | solution.py:62
  269.9 3.6 %fusion = (bf16[2,32,32,512]{3,2,1,0:T(8,128)(2,1)S(1)}, bf16[2,32,32,512]{3,2,1,0:T(8,128)(2,1)S(1)}) fusion(f32[1,32,32,512]{3,2,1,0:T(8,128)} %copy.87, f32[1,32,32,512]{3,2,1,0:T(8,128)} %copy.86, f32[1,32,32,512]{3,2,1,0:T(8,128)} %copy.93, f32[1,32,32,512]{3,2,1,0:T(8,128)S(1)} %copy.92), kind=kLoop, calls=%fused_computation.3 | loop fusion | flops 6291456 | bytes 12582912 | tf_op jit(solution)/shard_map/convert_element_type | solution.py:62
  275.2 1.4 fusion.2
  276.6 3.9 %pad_maximum_fusion = bf16[2,128,32,512]{3,2,1,0:T(8,128)(2,1)} fusion(bf16[2,32,32,512]{3,2,1,0:T(8,128)(2,1)S(1)} %get-tuple-element.22, bf16[2,32,32,512]{3,2,1,0:T(8,128)(2,1)S(1)} %get-tuple-element.21, bf16[2,32,32,512]{3,2,1,0:T(8,128)(2,1)S(1)} %get-tuple-element.20, bf16[2,32,32,512]{3,2,1,0:T(8,128)(2,1)S(1)} %get-tuple-element.19), kind=kLoop, calls=%fused_computation | loop fusion | flops 12582912 | bytes 16777216 | tf_op jit(solution)/shard_map/concatenate | solution.py:94
  (40 shorter events, 11.0 us)
Async XLA Ops:
  0.0 3.9 %copy-start = (f32[2,8,65]{2,1,0:T(8,128)S(1)}, f32[2,8,65]{2,1,0:T(8,128)}, u32[]{:S(2)}) copy-start(f32[2,8,65]{2,1,0:T(8,128)} %param.7) | copy-start | bytes 12484
  0.0 35.0 %collective-permute-start = (bf16[2,4,32,512]{3,2,1,0:T(8,128)(2,1)}, bf16[2,4,32,512]{3,2,1,0:T(8,128)(2,1)S(1)}, u32[]{:S(2)}, u32[]{:S(2)}) collective-permute-start(bf16[2,4,32,512]{3,2,1,0:T(8,128)(2,1)} %param.6), channel_id=1, source_target_pairs={{0,1},{1,2},{2,3},{3,4},{4,5},{5,6},{6,7},{7,8},{8,9},{9,10},{10,1... | collective-permute-start | bytes 786440 | tf_op jit(solution)/shard_map/ppermute | solution.py:22
  2.5 33.2 %collective-permute-start.1 = (bf16[2,4,32,512]{3,2,1,0:T(8,128)(2,1)}, bf16[2,4,32,512]{3,2,1,0:T(8,128)(2,1)S(1)}, u32[]{:S(2)}, u32[]{:S(2)}) collective-permute-start(bf16[2,4,32,512]{3,2,1,0:T(8,128)(2,1)} %param.6), channel_id=1, source_target_pairs={{1,0},{2,1},{3,2},{4,3},{5,4},{6,5},{7,6},{8,7},{9,8},{10,9},{11,1... | collective-permute-start | bytes 786440 | tf_op jit(solution)/shard_map/ppermute | solution.py:24
  4.9 8.0 %copy-start.7 = (s32[4]{0:T(128)S(1)}, s32[4]{0:T(128)}, u32[]{:S(2)}) copy-start(s32[4]{0:T(128)} %param.10) | copy-start | bytes 52
  4.9 8.7 %copy-start.6 = (bf16[2,4,32,512]{3,2,1,0:T(8,128)(2,1)S(1)}, bf16[2,4,32,512]{3,2,1,0:T(8,128)(2,1)}, u32[]{:S(2)}) copy-start(bf16[2,4,32,512]{3,2,1,0:T(8,128)(2,1)} %param.6) | copy-start | bytes 786436
  14.3 18.1 %copy-start.8 = (s32[4,32]{1,0:T(4,128)S(1)}, s32[4,32]{1,0:T(4,128)}, u32[]{:S(2)}) copy-start(s32[4,32]{1,0:T(4,128)} %param.9) | copy-start | bytes 1540
  14.3 20.7 %copy-start.9 = (s32[4,32]{1,0:T(4,128)S(1)}, s32[4,32]{1,0:T(4,128)}, u32[]{:S(2)}) copy-start(s32[4,32]{1,0:T(4,128)} %param.11) | copy-start | bytes 1540
  269.9 3.6 %copy-start.2 = (f32[1,32,32,512]{3,2,1,0:T(8,128)S(1)}, f32[1,32,32,512]{3,2,1,0:T(8,128)}, u32[]{:S(2)}) copy-start(f32[1,32,32,512]{3,2,1,0:T(8,128)} %copy.104) | copy-start | bytes 6291460
  269.9 4.1 %copy-start.3 = (f32[1,32,32,512]{3,2,1,0:T(8,128)S(1)}, f32[1,32,32,512]{3,2,1,0:T(8,128)}, u32[]{:S(2)}) copy-start(f32[1,32,32,512]{3,2,1,0:T(8,128)} %copy.105) | copy-start | bytes 6291460
  269.9 4.7 %copy-start.4 = (f32[1,32,32,512]{3,2,1,0:T(8,128)S(1)}, f32[1,32,32,512]{3,2,1,0:T(8,128)}, u32[]{:S(2)}) copy-start(f32[1,32,32,512]{3,2,1,0:T(8,128)} %copy.98) | copy-start | bytes 6291460
  269.9 5.3 %copy-start.5 = (f32[1,32,32,512]{3,2,1,0:T(8,128)S(1)}, f32[1,32,32,512]{3,2,1,0:T(8,128)}, u32[]{:S(2)}) copy-start(f32[1,32,32,512]{3,2,1,0:T(8,128)} %copy.99) | copy-start | bytes 6291460
  276.6 3.9 %copy-start.1 = (f32[2,8,65]{2,1,0:T(8,128)S(1)}, f32[2,8,65]{2,1,0:T(8,128)}, u32[]{:S(2)}) copy-start(f32[2,8,65]{2,1,0:T(8,128)} %param.7) | copy-start | bytes 12484
where the time goes:
time: 285 us; the launch traced here: 281 us
  matrix products  95.1 us (33%)
  local copies, waits for them, and re-layouts  81.1 us (28%)
  blocking collectives  78.1 us (27%)
  other arithmetic  19.4 us (7%)
  starting transfers between devices  3.83 us (1%)
  between operations  3.13 us (1%)
    psum x1, blocking collectives, body(): summed = lax.psum(stacked, 'chan').astype(jnp.bfloat16)  78.1 us
    another operation x8, local copies, waits for them, and re-layouts, cross_block(): return (jnp.stack([real_out, imag_out]) / WIN).astype(jnp.bfloat16)  52.2 us
    dot_general x1, matrix products, velocity_whiten(): jnp.einsum('pfok,qwkf->pqwof', banded, padded, precision=lax.Precision.HI...  49.4 us
    dot_general x1, local copies, waits for them, and re-layouts, velocity_whiten(): jnp.einsum('okt,ptf->pfok', shifter, taps, precision=lax.Precision.HIGHEST)  18 us
    dot_general x4, matrix products, cross_block(): jnp.einsum('pwsf,pwcf->scf', source, swapped, preferred_element_type=jnp....  17.4 us
    dot_general x4, matrix products, cross_block(): jnp.einsum('pwsf,pwcf->scf', source, whitened, preferred_element_type=jnp...  17.2 us
    dot_general x1, matrix products, velocity_whiten(): jnp.einsum('okt,ptf->pfok', shifter, taps, precision=lax.Precision.HIGHEST)  8.01 us
  transfers between devices with their start and end apart: 2, of which 0 were waited for; matrix products, arithmetic and copies ran while one was open for 10% of the time, Pallas kernels for 0%

commit v1 on v0

--- a/solution.py
+++ b/solution.py
@@ -88,7 +88,7 @@
             for round_pos in range(ROUNDS)
         ]
     )
-    summed = lax.psum(stacked, "chan").astype(jnp.bfloat16)
+    summed = jnp.sum(lax.all_gather(stacked, "chan"), axis=0).astype(jnp.bfloat16)
     for round_pos in range(ROUNDS):
         blocks.append(cross_block(summed[round_pos], whitened, swapped))
     return jnp.concatenate(blocks, axis=1)

time: 285 us -> 397 us (1.39)
  waiting for transfers between devices: 0.01 us -> 173 us
  blocking collectives: 78.1 us -> 0 us
  between operations: 3.13 us -> 16.5 us
  other arithmetic: 19.4 us -> 31.9 us
  matrix products: 95.1 us -> 84.2 us
    all_gather x0 -> x1, waiting for transfers between devices: none -> 173 us  [body(): lax.all_gather(stacked, 'chan')]
    psum x1 -> x0, blocking collectives: 78.1 us -> none  [body(): summed = lax.psum(stacked, 'chan').astype(jnp.bfloat16)]
    reduce_sum x0 -> x1, other arithmetic: none -> 12.9 us  [body(): jnp.sum(lax.all_gather(stacked, 'chan'), axis=0).astype(jnp.bfloat16)]
    dot_general x1, matrix products: 49.4 us -> 38.2 us  [velocity_whiten(): jnp.einsum('pfok,qwkf->pqwof', banded, padded, precision=lax.Precision.HI...]
    reduce_sum x0 -> x1, local copies, waits for them, and re-layouts: none -> 4.66 us  [body(): jnp.sum(lax.all_gather(stacked, 'chan'), axis=0).astype(jnp.bfloat16)]
  transfers between devices with their start and end apart: 2 -> 3, of which waited for: 0 -> 1; matrix products, arithmetic and copies ran while one was open for 10% -> 7% of each run, Pallas kernels for 0% -> 0%
where the time goes in v1:
time: 397 us; the launch traced here: 392 us
  waiting for transfers between devices  173 us (44%)
  matrix products  84.2 us (21%)
  local copies, waits for them, and re-layouts  82.7 us (21%)
  other arithmetic  31.9 us (8%)
  between operations  16.5 us (4%)
    all_gather x1, waiting for transfers between devices, body(): lax.all_gather(stacked, 'chan')  173 us
    another operation x8, local copies, waits for them, and re-layouts, cross_block(): return (jnp.stack([real_out, imag_out]) / WIN).astype(jnp.bfloat16)  52.2 us
    dot_general x1, matrix products, velocity_whiten(): jnp.einsum('pfok,qwkf->pqwof', banded, padded, precision=lax.Precision.HI...  38.2 us
    dot_general x1, local copies, waits for them, and re-layouts, velocity_whiten(): jnp.einsum('okt,ptf->pfok', shifter, taps, precision=lax.Precision.HIGHEST)  18.1 us
    dot_general x4, matrix products, cross_block(): jnp.einsum('pwsf,pwcf->scf', source, whitened, preferred_element_type=jnp...  17.5 us
    dot_general x4, matrix products, cross_block(): jnp.einsum('pwsf,pwcf->scf', source, swapped, preferred_element_type=jnp....  17.4 us
    reduce_sum x1, other arithmetic, body(): jnp.sum(lax.all_gather(stacked, 'chan'), axis=0).astype(jnp.bfloat16)  12.9 us
    dot_general x1, matrix products, velocity_whiten(): jnp.einsum('okt,ptf->pfok', shifter, taps, precision=lax.Precision.HIGHEST)  8 us
  transfers between devices with their start and end apart: 3, of which 1 were waited for; matrix products, arithmetic and copies ran while one was open for 7% of the time, Pallas kernels for 0%

profile of v1, /device:TPU:0, one launch (start us, length us, event | category | flops | bytes accessed | tf_op | source)
XLA Modules:
  0.0 391.9 jit_solution(4462330221985043085)
XLA Ops:
  6.5 2.5 collective-permute-start
  9.1 1.3 collective-permute-start.1
  11.5 8.0 %convolution_bitcast_fusion = f32[2,512,32,96,1]{1,3,2,0,4:T(8,128)} fusion(f32[2,65,512,1]{2,1,3,0:T(8,128)S(1)} %convolution_bitcast_fusion.10, s32[32,96]{1,0:T(8,128)S(1)} %iota_subtract_fusion), kind=kOutput, calls=%fused_computation.1 | convolution fusion | flops 2453867520 | bytes 12861440 | tf_op jit(solution)/shard_map/okt,ptf->pfok/dot_general | solution.py:46
  23.4 18.1 %copy.86 = f32[2,512,32,96,1]{3,2,0,4,1:T(8,128)} copy(f32[2,512,32,96,1]{1,3,2,0,4:T(8,128)} %convolution_bitcast_fusion) | data formatting | bytes 25165824 | tf_op jit(solution)/shard_map/okt,ptf->pfok/dot_general | solution.py:46
  42.9 38.2 %convolution_bitcast_fusion.9 = f32[2,2,4,32,512]{3,2,0,1,4:T(4,128)} fusion(f32[2,512,32,96,1]{3,2,0,4,1:T(8,128)} %copy.86, bf16[2,4,32,512]{2,1,0,3:T(4,128)(2,1)S(1)} %copy.57, bf16[2,4,32,512]{2,1,0,3:T(4,128)(2,1)S(1)} %copy.56, bf16[2,4,32,512]{2,1,0,3:T(4,128)(2,1)S(1)} %copy.55), kind=kOutput, calls=%fused_computation.18 | convolution fusion | flops 304349184 | bytes 14417920 | tf_op jit(solution)/shard_map/pfok,qwkf->pqwof/dot_general | solution.py:47
  81.1 2.7 multiply_add_fusion
  85.3 2.1 fusion.40
  87.4 2.4 fusion.58
  92.4 1.5 pad_maximum_fusion.1
  93.9 172.8 %all-gather.3.cloned.1.call-done = f32[64,2,4,32,512]{4,3,2,1,0:T(8,128)} async-done(((f32[4,2,4,32,512]{4,3,2,1,0:T(8,128)}), f32[64,2,4,32,512]{4,3,2,1,0:T(8,128)}) %all-gather.3.cloned.1.call-update) | async-done | bytes 33554448 | tf_op jit(solution)/shard_map/all_gather | solution.py:91
  266.7 12.9 %reduce_sum.9 = bf16[4,2,4,32,512]{4,3,2,1,0:T(8,128)(2,1)S(1)} reduce(f32[16,4,2,4,32,512]{5,4,3,2,1,0:T(8,128)} %bitcast.174, f32[]{:T(128)} %constant.17.clone.1), dimensions={0}, to_apply=%region_0.1 | reduce | flops 7864320 | bytes 34603012 | tf_op jit(solution)/shard_map/reduce_sum | solution.py:91
  279.6 4.7 %copy.67 = bf16[4,2,4,32,512]{3,2,1,4,0:T(4,128)(2,1)} copy(bf16[4,2,4,32,512]{4,3,2,1,0:T(8,128)(2,1)S(1)} %reduce_sum.9) | data formatting | bytes 2097152 | tf_op jit(solution)/shard_map/reduce_sum | solution.py:91
  284.2 3.0 slice_bitcast_fusion.3
  287.2 4.3 %convolution_bitcast_fusion.8 = f32[1,32,32,512]{1,2,3,0:T(8,128)} fusion(bf16[2,4,32,512]{2,1,0,3:T(4,128)(2,1)S(1)} %get-tuple-element.7, bf16[1,4,32,512]{2,1,3,0:T(4,128)(2,1)S(1)} %fusion.40, bf16[1,4,32,512]{2,1,3,0:T(4,128)(2,1)S(1)} %get-tuple-element.6), kind=kOutput, calls=%fused_computation.17 | convolution fusion | flops 8912896 | bytes 2621440 | tf_op jit(solution)/shard_map/pwsf,pwcf->scf/dot_general | solution.py:60
  291.5 4.3 %convolution_bitcast_fusion.7 = f32[1,32,32,512]{1,2,3,0:T(8,128)} fusion(bf16[2,4,32,512]{2,1,0,3:T(4,128)(2,1)S(1)} %get-tuple-element.7, bf16[1,4,32,512]{2,1,3,0:T(4,128)(2,1)S(1)} %get-tuple-element.5, bf16[1,4,32,512]{2,1,3,0:T(4,128)(2,1)S(1)} %fusion.40), kind=kOutput, calls=%fused_computation.16 | convolution fusion | flops 8912896 | bytes 2621440 | tf_op jit(solution)/shard_map/pwsf,pwcf->scf/dot_general | solution.py:61
  295.8 4.5 %convolution_bitcast_fusion.3 = f32[1,32,32,512]{1,2,3,0:T(8,128)} fusion(bf16[2,4,32,512]{2,1,0,3:T(4,128)(2,1)S(1)} %get-tuple-element.8, bf16[1,4,32,512]{2,1,3,0:T(4,128)(2,1)S(1)} %get-tuple-element.5, bf16[1,4,32,512]{2,1,3,0:T(4,128)(2,1)S(1)} %fusion.40), kind=kOutput, calls=%fused_computation.12 | convolution fusion | flops 8912896 | bytes 2621440 | tf_op jit(solution)/shard_map/pwsf,pwcf->scf/dot_general | solution.py:61
  300.3 4.3 %convolution_bitcast_fusion.4 = f32[1,32,32,512]{1,2,3,0:T(8,128)} fusion(bf16[2,4,32,512]{2,1,0,3:T(4,128)(2,1)S(1)} %get-tuple-element.8, bf16[1,4,32,512]{2,1,3,0:T(4,128)(2,1)S(1)} %fusion.40, bf16[1,4,32,512]{2,1,3,0:T(4,128)(2,1)S(1)} %get-tuple-element.6), kind=kOutput, calls=%fused_computation.13 | convolution fusion | flops 8912896 | bytes 2621440 | tf_op jit(solution)/shard_map/pwsf,pwcf->scf/dot_general | solution.py:60
  304.6 4.3 %convolution_bitcast_fusion.5 = f32[1,32,32,512]{1,2,3,0:T(8,128)} fusion(bf16[2,4,32,512]{2,1,0,3:T(4,128)(2,1)S(1)} %get-tuple-element.9, bf16[1,4,32,512]{2,1,3,0:T(4,128)(2,1)S(1)} %get-tuple-element.5, bf16[1,4,32,512]{2,1,3,0:T(4,128)(2,1)S(1)} %fusion.40), kind=kOutput, calls=%fused_computation.14 | convolution fusion | flops 8912896 | bytes 2621440 | tf_op jit(solution)/shard_map/pwsf,pwcf->scf/dot_general | solution.py:61
  308.9 4.3 %convolution_bitcast_fusion.6 = f32[1,32,32,512]{1,2,3,0:T(8,128)} fusion(bf16[2,4,32,512]{2,1,0,3:T(4,128)(2,1)S(1)} %get-tuple-element.9, bf16[1,4,32,512]{2,1,3,0:T(4,128)(2,1)S(1)} %fusion.40, bf16[1,4,32,512]{2,1,3,0:T(4,128)(2,1)S(1)} %get-tuple-element.6), kind=kOutput, calls=%fused_computation.15 | convolution fusion | flops 8912896 | bytes 2621440 | tf_op jit(solution)/shard_map/pwsf,pwcf->scf/dot_general | solution.py:60
  313.2 4.5 %convolution_bitcast_fusion.2 = f32[1,32,32,512]{1,2,3,0:T(8,128)} fusion(bf16[2,4,32,512]{2,1,0,3:T(4,128)(2,1)S(1)} %get-tuple-element.10, bf16[1,4,32,512]{2,1,3,0:T(4,128)(2,1)S(1)} %fusion.40, bf16[1,4,32,512]{2,1,3,0:T(4,128)(2,1)S(1)} %get-tuple-element.6), kind=kOutput, calls=%fused_computation.11 | convolution fusion | flops 8912896 | bytes 2621440 | tf_op jit(solution)/shard_map/pwsf,pwcf->scf/dot_general | solution.py:60
  317.7 4.3 %convolution_bitcast_fusion.1 = f32[1,32,32,512]{1,2,3,0:T(8,128)} fusion(bf16[2,4,32,512]{2,1,0,3:T(4,128)(2,1)S(1)} %get-tuple-element.10, bf16[1,4,32,512]{2,1,3,0:T(4,128)(2,1)S(1)} %get-tuple-element.5, bf16[1,4,32,512]{2,1,3,0:T(4,128)(2,1)S(1)} %fusion.40), kind=kOutput, calls=%fused_computation.10 | convolution fusion | flops 8912896 | bytes 2621440 | tf_op jit(solution)/shard_map/pwsf,pwcf->scf/dot_general | solution.py:61
  322.0 6.6 %copy.71 = f32[1,32,32,512]{3,2,1,0:T(8,128)} copy(f32[1,32,32,512]{1,2,3,0:T(8,128)} %convolution_bitcast_fusion.7) | data formatting | bytes 4194304 | tf_op jit(solution)/shard_map/stack | solution.py:62
  328.6 6.6 %copy.70 = f32[1,32,32,512]{3,2,1,0:T(8,128)} copy(f32[1,32,32,512]{1,2,3,0:T(8,128)} %convolution_bitcast_fusion.8) | data formatting | bytes 4194304 | tf_op jit(solution)/shard_map/stack | solution.py:62
  335.3 5.8 %copy.79 = f32[1,32,32,512]{3,2,1,0:T(8,128)S(1)} copy(f32[1,32,32,512]{1,2,3,0:T(8,128)} %convolution_bitcast_fusion.3) | data formatting | bytes 4194304 | tf_op jit(solution)/shard_map/stack | solution.py:62
  341.1 6.6 %copy.78 = f32[1,32,32,512]{3,2,1,0:T(8,128)} copy(f32[1,32,32,512]{1,2,3,0:T(8,128)} %convolution_bitcast_fusion.4) | data formatting | bytes 4194304 | tf_op jit(solution)/shard_map/stack | solution.py:62
  347.7 6.7 %copy.75 = f32[1,32,32,512]{3,2,1,0:T(8,128)} copy(f32[1,32,32,512]{1,2,3,0:T(8,128)} %convolution_bitcast_fusion.5) | data formatting | bytes 4194304 | tf_op jit(solution)/shard_map/stack | solution.py:62
  354.3 6.6 %copy.74 = f32[1,32,32,512]{3,2,1,0:T(8,128)} copy(f32[1,32,32,512]{1,2,3,0:T(8,128)} %convolution_bitcast_fusion.6) | data formatting | bytes 4194304 | tf_op jit(solution)/shard_map/stack | solution.py:62
  360.9 6.6 %copy.82 = f32[1,32,32,512]{3,2,1,0:T(8,128)} copy(f32[1,32,32,512]{1,2,3,0:T(8,128)} %convolution_bitcast_fusion.2) | data formatting | bytes 4194304 | tf_op jit(solution)/shard_map/stack | solution.py:62
  367.6 6.6 %copy.83 = f32[1,32,32,512]{3,2,1,0:T(8,128)} copy(f32[1,32,32,512]{1,2,3,0:T(8,128)} %convolution_bitcast_fusion.1) | data formatting | bytes 4194304 | tf_op jit(solution)/shard_map/stack | solution.py:62
  374.2 4.2 %fusion = (bf16[2,32,32,512]{3,2,1,0:T(8,128)(2,1)S(1)}, bf16[2,32,32,512]{3,2,1,0:T(8,128)(2,1)S(1)}) fusion(f32[1,32,32,512]{3,2,1,0:T(8,128)} %copy.71, f32[1,32,32,512]{3,2,1,0:T(8,128)} %copy.70, f32[1,32,32,512]{3,2,1,0:T(8,128)} %copy.75, f32[1,32,32,512]{3,2,1,0:T(8,128)} %copy.74), kind=kLoop, calls=%fused_computation.3 | loop fusion | flops 6291456 | bytes 12582912 | tf_op jit(solution)/shard_map/convert_element_type | solution.py:62
  379.5 1.3 fusion.2
  380.9 3.9 pad_maximum_fusion
  (38 shorter events, 8.9 us)
Async XLA Ops:
  6.5 3.9 copy-start
  6.5 260.1 %all-gather.3.cloned.1.call-start = ((), (), s32[]{:S(2)}) async-start(), calls=%async_computation | async-start | bytes 35651584 | tf_op jit(solution)/shard_map/all_gather | solution.py:91
  6.5 35.7 %collective-permute-start = (bf16[2,4,32,512]{3,2,1,0:T(8,128)(2,1)}, bf16[2,4,32,512]{3,2,1,0:T(8,128)(2,1)S(1)}, u32[]{:S(2)}, u32[]{:S(2)}) collective-permute-start(bf16[2,4,32,512]{3,2,1,0:T(8,128)(2,1)} %param.6), channel_id=1, source_target_pairs={{0,1},{1,2},{2,3},{3,4},{4,5},{5,6},{6,7},{7,8},{8,9},{9,10},{10,1... | collective-permute-start | bytes 786440 | tf_op jit(solution)/shard_map/ppermute | solution.py:22
  9.1 32.4 %collective-permute-start.1 = (bf16[2,4,32,512]{3,2,1,0:T(8,128)(2,1)}, bf16[2,4,32,512]{3,2,1,0:T(8,128)(2,1)S(1)}, u32[]{:S(2)}, u32[]{:S(2)}) collective-permute-start(bf16[2,4,32,512]{3,2,1,0:T(8,128)(2,1)} %param.6), channel_id=1, source_target_pairs={{1,0},{2,1},{3,2},{4,3},{5,4},{6,5},{7,6},{8,7},{9,8},{10,9},{11,1... | collective-permute-start | bytes 786440 | tf_op jit(solution)/shard_map/ppermute | solution.py:24
  11.4 8.0 %copy-start.6 = (s32[4]{0:T(128)S(1)}, s32[4]{0:T(128)}, u32[]{:S(2)}) copy-start(s32[4]{0:T(128)} %param.10) | copy-start | bytes 52
  11.4 8.7 %copy-start.5 = (bf16[2,4,32,512]{3,2,1,0:T(8,128)(2,1)S(1)}, bf16[2,4,32,512]{3,2,1,0:T(8,128)(2,1)}, u32[]{:S(2)}) copy-start(bf16[2,4,32,512]{3,2,1,0:T(8,128)(2,1)} %param.6) | copy-start | bytes 786436
  11.4 9.4 %copy-start.7 = (s32[4,32]{1,0:T(4,128)S(1)}, s32[4,32]{1,0:T(4,128)}, u32[]{:S(2)}) copy-start(s32[4,32]{1,0:T(4,128)} %param.9) | copy-start | bytes 1540
  23.4 18.1 %copy-start.8 = (s32[4,32]{1,0:T(4,128)S(1)}, s32[4,32]{1,0:T(4,128)}, u32[]{:S(2)}) copy-start(s32[4,32]{1,0:T(4,128)} %param.11) | copy-start | bytes 1540
  374.2 4.2 %copy-start.2 = (f32[1,32,32,512]{3,2,1,0:T(8,128)S(1)}, f32[1,32,32,512]{3,2,1,0:T(8,128)}, u32[]{:S(2)}) copy-start(f32[1,32,32,512]{3,2,1,0:T(8,128)} %copy.78) | copy-start | bytes 6291460
  374.2 4.7 %copy-start.3 = (f32[1,32,32,512]{3,2,1,0:T(8,128)S(1)}, f32[1,32,32,512]{3,2,1,0:T(8,128)}, u32[]{:S(2)}) copy-start(f32[1,32,32,512]{3,2,1,0:T(8,128)} %copy.82) | copy-start | bytes 6291460
  374.2 5.3 %copy-start.4 = (f32[1,32,32,512]{3,2,1,0:T(8,128)S(1)}, f32[1,32,32,512]{3,2,1,0:T(8,128)}, u32[]{:S(2)}) copy-start(f32[1,32,32,512]{3,2,1,0:T(8,128)} %copy.83) | copy-start | bytes 6291460
  380.9 3.9 copy-start.1
Sparse Core Ops, SparseCore 0:
  94.0 172.6 all-gather.2
